TPU v7x, 32 devices: a whole 2x2x4 slice. The times are simulated.
32 devices in a mesh: seq: 16 (over z, y, core), chan: 2 (over x).
Axes of the slice: x: 2, y: 2, z: 4, core: 2. Of those that a mesh axis runs over, the one named last changes fastest.
Arguments:
- inputs: bfloat16 [512, 512, 512], P('chan', 'seq'), may hold values from -6 to 6
- gate_in: bfloat16 [512, 512, 512], P('chan', 'seq'), may hold values from -6 to 6
- gate_out: bfloat16 [512, 512, 512], P('seq', 'chan'), may hold values from -6 to 6
- cotangent: bfloat16 [512, 512, 512], P('seq', 'chan'), may hold values from -6 to 6
- mix_one: bfloat16 [512, 512, 512], P('seq', 'chan'), may hold values from -6 to 6
- second_mixing_blocks: bfloat16 [512, 512, 512], P('seq', 'chan'), may hold values from -6 to 6
Outputs:
- grad_input: bfloat16 [512, 512, 512], P('chan', 'seq')
- grad_gate_out: bfloat16 [512, 512, 512], P('seq', 'chan')
- grad_mix_one: bfloat16 [512, 512, 512], P('seq', 'chan')
- grad_mix_two: bfloat16 [512, 512, 512], P('seq', 'chan')
All inputs are finite; a program needn't handle non-finite values.
Results may differ from a plain program's by a relative error of at most 0.0095.
Values may be sent and summed in bfloat16 or wider, within the bound.
A program may use at most 256 MiB of HBM per device.

v0:
```python
import math
import jax
import jax.numpy as jnp
from jax import lax
from jax.sharding import PartitionSpec as P


def shards(inputs, gate_in, gate_out, cotangent, mix_one, second_mixing_blocks):
    chan_count = lax.axis_size("chan")
    first_scale = 1.0 / math.sqrt(mix_one.shape[2])
    scale_two = 1.0 / math.sqrt(second_mixing_blocks.shape[2])
    gated = (inputs.astype(jnp.float32) * gate_in.astype(jnp.float32)).astype(jnp.bfloat16)
    grad_second = (cotangent.astype(jnp.float32) * gate_out.astype(jnp.float32)).astype(
        jnp.bfloat16
    )
    gated_all = lax.all_gather(gated, "chan", axis=0, tiled=True)
    full_one, full_two = (
        lax.all_gather(mix_one, "chan", axis=1, tiled=True),
        lax.all_gather(second_mixing_blocks, "chan", axis=1, tiled=True),
    )
    first = (
        jnp.einsum("roi,dri->odr", full_one, gated, preferred_element_type=jnp.float32)
        * first_scale
    ).astype(jnp.bfloat16)
    first_cols = lax.all_to_all(first, "seq", split_axis=0, concat_axis=2, tiled=True)
    first_all = lax.all_gather(first_cols, "chan", axis=1, tiled=True)
    second = (
        jnp.einsum("coi,cdi->cdo", full_two, first_cols, preferred_element_type=jnp.float32)
        * scale_two
    ).astype(jnp.bfloat16)
    grad_gate_out = (cotangent.astype(jnp.float32) * second.astype(jnp.float32)).astype(
        jnp.bfloat16
    )
    grad_first_cols = (
        jnp.einsum("coi,cdo->cdi", full_two, grad_second, preferred_element_type=jnp.float32)
        * scale_two
    ).astype(jnp.bfloat16)
    grad_second_rows = lax.all_to_all(grad_second, "chan", split_axis=2, concat_axis=1, tiled=True)
    grad_mix_two = (
        jnp.einsum("cdo,cdi->coi", grad_second_rows, first_all, preferred_element_type=jnp.float32)
        * scale_two
    ).astype(jnp.bfloat16)
    grad_first = lax.all_to_all(grad_first_cols, "seq", split_axis=2, concat_axis=0, tiled=True)
    grad_part = lax.all_to_all(grad_first, "chan", split_axis=0, concat_axis=1, tiled=True)
    grad_mix_one = (
        jnp.einsum("odr,dri->roi", grad_part, gated_all, preferred_element_type=jnp.float32)
        * first_scale
    ).astype(jnp.bfloat16)
    rows_here, columns, _ = full_one.shape
    group_weight = full_one.reshape(rows_here, chan_count, columns // chan_count, columns)
    group_grad = grad_first.reshape(
        chan_count, columns // chan_count, grad_first.shape[1], rows_here
    )
    summand_terms = (
        jnp.einsum("rgoi,godr->gdri", group_weight, group_grad, preferred_element_type=jnp.float32)
        * first_scale
    ).astype(jnp.bfloat16)
    grad_gated = jnp.sum(summand_terms.astype(jnp.float32), axis=0).astype(jnp.bfloat16)
    grad_input = (grad_gated.astype(jnp.float32) * gate_in.astype(jnp.float32)).astype(jnp.bfloat16)
    return (grad_input, grad_gate_out, grad_mix_one, grad_mix_two)


def solution(mesh):
    return jax.shard_map(
        shards,
        mesh=mesh,
        in_specs=(
            P("chan", "seq", None),
            P("chan", "seq", None),
            P("seq", "chan", None),
            P("seq", "chan", None),
            P("seq", "chan", None),
            P("seq", "chan", None),
        ),
        out_specs=(
            P("chan", "seq", None),
            P("seq", "chan", None),
            P("seq", "chan", None),
            P("seq", "chan", None),
        ),
        check_vma=False,
    )
```

profile of v0, /device:TPU:0, one launch (start us, length us, event | category | flops | bytes accessed | tf_op | source)
XLA Modules:
  0.0 1185.1 jit_solution(13639298940770544008)
XLA Ops:
  7.2 0.0 all-gather.5.cloned.1.call-start
  7.2 0.7 all-gather.5.cloned.1.call-update
  7.9 0.0 all-gather.7.cloned.1.call-start
  7.9 0.7 all-gather.7.cloned.1.call-update
  8.6 0.0 all-gather.9.cloned.1.call-start
  8.7 9.9 fusion
  18.6 192.5 %all-gather.5.cloned.1.call-done = bf16[32,512,512]{2,1,0:T(8,128)(2,1)} async-done(((bf16[32,256,512]{2,1,0:T(8,128)(2,1)}), bf16[32,512,512]{2,1,0:T(8,128)(2,1)}) %all-gather.5.cloned.1.call-update) | async-done | bytes 16777232 | tf_op jit(solution)/shard_map/all_gather | solution.py:19
  211.1 15.1 %multiply_convert_fusion.5 = bf16[32,256,512]{2,1,0:T(8,128)(2,1)} fusion(bf16[32,256,512]{2,1,0:T(8,128)(2,1)} %fusion, bf16[32,512,512]{2,1,0:T(8,128)(2,1)} %all-gather.5.cloned.1.call-done), kind=kOutput, calls=%fused_computation.14 | convolution fusion | flops 4303355904 | bytes 33554432 | tf_op jit(solution)/shard_map/coi,cdo->cdi/dot_general | solution.py:35
  226.2 15.2 %copy.29 = bf16[32,256,512]{1,0,2:T(8,128)(2,1)} copy(bf16[32,256,512]{2,1,0:T(8,128)(2,1)} %multiply_convert_fusion.5) | data formatting | bytes 16777216 | tf_op jit(solution)/shard_map/convert_element_type | solution.py:37
  241.4 188.0 %all_to_all.72 = bf16[32,256,512]{1,0,2:T(8,128)(2,1)} all-to-all(bf16[32,256,512]{1,0,2:T(8,128)(2,1)} %copy.29), channel_id=1, replica_groups=mesh['seq'=16,'chan'=2] {'seq'}, dimensions={2} | all-to-all | bytes 16777216 | tf_op jit(solution)/shard_map/all_to_all | solution.py:43
  429.4 12.5 %copy.31 = bf16[16,32,256,32]{2,3,1,0:T(8,128)(2,1)} copy(bf16[16,32,256,32]{2,1,3,0:T(8,128)(2,1)} %bitcast.42) | data formatting | bytes 16777216 | tf_op jit(solution)/shard_map/all_to_all | solution.py:43
  441.8 0.0 all-gather.7.cloned.1.call-done
  441.8 26.4 %fusion.7 = bf16[32,256,512]{2,1,0:T(8,128)(2,1)} fusion(bf16[32,2,256,512]{3,2,1,0:T(8,128)(2,1)} %bitcast.45, bf16[2,256,256,32]{2,3,1,0:T(8,128)(2,1)} %bitcast.39), kind=kOutput, calls=%fused_computation.18 | convolution fusion | flops 4315938816 | bytes 33554432 | tf_op jit(solution)/shard_map/rgoi,godr->gdri/dot_general | solution.py:55
  468.2 18.1 %fusion.3 = (bf16[256,32,512]{2,0,1:T(8,128)(2,1)}, bf16[256,32,512]{2,0,1:T(8,128)(2,1)}) fusion(bf16[256,32,512]{2,1,0:T(8,128)(2,1)} %param.6, bf16[256,32,512]{2,1,0:T(8,128)(2,1)} %param.7, bf16[32,256,512]{2,1,0:T(8,128)(2,1)} %fusion.7), kind=kLoop, calls=%fused_computation.8 | loop fusion | flops 29360128 | bytes 41943040 | tf_op jit(solution)/shard_map/convert_element_type | solution.py:12
  486.4 0.0 all-gather.9.cloned.1.call-update
  486.4 0.0 all-gather.11.cloned.1.call-start
  486.5 16.1 %fusion.6 = bf16[512,256,32]{0,1,2:T(8,128)(2,1)} fusion(bf16[256,32,512]{2,0,1:T(8,128)(2,1)} %get-tuple-element.16, bf16[32,512,512]{2,1,0:T(8,128)(2,1)} %all-gather.7.cloned.1.call-done), kind=kOutput, calls=%fused_computation.17 | convolution fusion | flops 4303355904 | bytes 33554432 | tf_op jit(solution)/shard_map/roi,dri->odr/dot_general | solution.py:22
  502.6 15.2 %copy.36 = bf16[512,256,32]{1,2,0:T(8,128)(2,1)} copy(bf16[512,256,32]{0,1,2:T(8,128)(2,1)} %fusion.6) | data formatting | bytes 16777216 | tf_op jit(solution)/shard_map/convert_element_type | solution.py:24
  517.8 187.7 %all_to_all.73 = bf16[512,256,32]{1,2,0:T(8,128)(2,1)} all-to-all(bf16[512,256,32]{1,2,0:T(8,128)(2,1)} %copy.36), channel_id=1, replica_groups=mesh['seq'=16,'chan'=2] {'seq'}, dimensions={0} | all-to-all | bytes 16777216 | tf_op jit(solution)/shard_map/all_to_all | solution.py:25
  705.5 8.0 copy.37
  713.5 12.0 %copy.43 = bf16[32,256,512]{2,1,0:T(8,128)(2,1)} copy(bf16[32,256,512]{1,2,0:T(8,128)(2,1)} %bitcast.37) | data formatting | bytes 16777216 | tf_op jit(solution)/shard_map/all_to_all | solution.py:25
  725.5 0.0 all-gather.11.cloned.1.call-update
  725.5 15.3 %copy.41 = bf16[32,256,512]{1,0,2:T(8,128)(2,1)} copy(bf16[32,256,512]{2,1,0:T(8,128)(2,1)} %fusion) | data formatting | bytes 16777216 | tf_op jit(solution)/shard_map/convert_element_type | solution.py:13
  740.8 195.0 %all_to_all.74 = bf16[32,256,512]{1,0,2:T(8,128)(2,1)} all-to-all(bf16[32,256,512]{1,0,2:T(8,128)(2,1)} %copy.41), channel_id=1, replica_groups=mesh['seq'=16,'chan'=2] {'chan'}, dimensions={2} | all-to-all | bytes 16777216 | tf_op jit(solution)/shard_map/all_to_all | solution.py:38
  935.8 7.0 all-to-all-start.2
  942.8 16.7 %copy.60 = bf16[32,256,2,256]{1,2,3,0:T(2,128)(2,1)} copy(bf16[32,256,2,256]{1,0,3,2:T(8,128)(2,1)} %bitcast.41) | data formatting | bytes 16777216 | tf_op jit(solution)/shard_map/all_to_all | solution.py:38
  959.5 14.1 %all_to_all.67 = bf16[32,512,256]{1,2,0:T(8,128)(2,1)} reshape(bf16[32,2,256,256]{2,1,3,0:T(2,128)(2,1)} %bitcast.44) | data formatting | bytes 16777216 | tf_op jit(solution)/shard_map/all_to_all | solution.py:38
  973.6 11.5 copy.44
  985.1 119.2 %all-to-all-done.2 = bf16[512,256,32]{1,2,0:T(8,128)(2,1)} async-done(((bf16[512,256,32]{1,2,0:T(8,128)(2,1)}), bf16[512,256,32]{1,2,0:T(8,128)(2,1)}, u32[]{:S(2)}, u32[]{:S(2)}) %all-to-all-start.2) | async-done | bytes 8388640 | tf_op jit(solution)/shard_map/all_to_all | solution.py:44
  1104.3 16.5 %copy.40 = bf16[256,2,256,32]{2,1,0,3:T(2,128)(2,1)} copy(bf16[256,2,256,32]{2,3,0,1:T(8,128)(2,1)} %bitcast.14) | data formatting | bytes 16777216 | tf_op jit(solution)/shard_map/all_to_all | solution.py:44
  1120.8 14.1 %all_to_all.63 = bf16[256,512,32]{1,0,2:T(8,128)(2,1)} reshape(bf16[256,2,256,32]{2,1,0,3:T(2,128)(2,1)} %copy.40) | data formatting | bytes 16777216 | tf_op jit(solution)/shard_map/all_to_all | solution.py:44
  1134.8 15.6 %fusion.1 = bf16[32,256,512]{2,1,0:T(8,128)(2,1)} fusion(bf16[32,256,512]{2,1,0:T(8,128)(2,1)} %param.9, bf16[32,256,512]{1,2,0:T(8,128)(2,1)} %bitcast.38, bf16[32,512,512]{2,1,0:T(8,128)(2,1)} %all-gather.5.cloned.1.call-done), kind=kOutput, calls=%fused_computation.6 | convolution fusion | flops 4320133120 | bytes 41943040 | tf_op jit(solution)/shard_map/coi,cdi->cdo/dot_general | solution.py:28
  1150.5 0.0 all-gather.9.cloned.1.call-done
  1150.5 14.0 %multiply_convert_fusion.2 = bf16[32,256,512]{2,1,0:T(8,128)(2,1)} fusion(bf16[256,512,32]{1,0,2:T(8,128)(2,1)} %all_to_all.63, bf16[512,32,512]{2,0,1:T(8,128)(2,1)} %all-gather.9.cloned.1.call-done), kind=kOutput, calls=%fused_computation.11 | convolution fusion | flops 4303355904 | bytes 33554432 | tf_op jit(solution)/shard_map/odr,dri->roi/dot_general | solution.py:46
  1164.5 0.0 all-gather.11.cloned.1.call-done
  1164.5 13.8 %multiply_convert_fusion.1 = bf16[32,256,512]{2,1,0:T(8,128)(2,1)} fusion(bf16[32,512,256]{1,2,0:T(8,128)(2,1)} %all_to_all.67, bf16[32,512,512]{2,1,0:T(8,128)(2,1)} %all-gather.11.cloned.1.call-done), kind=kOutput, calls=%fused_computation.10 | convolution fusion | flops 4303355904 | bytes 33554432 | tf_op jit(solution)/shard_map/cdo,cdi->coi/dot_general | solution.py:40
Async XLA Ops:
  7.2 204.0 %all-gather.5.cloned.1.call-start = ((), (), s32[]{:S(2)}) async-start(), calls=%async_computation.4 | async-start | bytes 25165824 | tf_op jit(solution)/shard_map/all_gather | solution.py:19
  7.9 433.9 %all-gather.7.cloned.1.call-start = ((), (), s32[]{:S(2)}) async-start(), calls=%async_computation.5 | async-start | bytes 25165824 | tf_op jit(solution)/shard_map/all_gather | solution.py:18
  8.6 1141.8 %all-gather.9.cloned.1.call-start = ((), (), s32[]{:S(2)}) async-start(), calls=%async_computation.6 | async-start | bytes 25165824 | tf_op jit(solution)/shard_map/all_gather | solution.py:16
  486.4 678.1 %all-gather.11.cloned.1.call-start = ((), (), s32[]{:S(2)}) async-start(), calls=%async_computation.7 | async-start | bytes 25165824 | tf_op jit(solution)/shard_map/all_gather | solution.py:26
  935.8 168.5 %all-to-all-start.2 = ((bf16[512,256,32]{1,2,0:T(8,128)(2,1)}), bf16[512,256,32]{1,2,0:T(8,128)(2,1)}, u32[]{:S(2)}, u32[]{:S(2)}) async-start(bf16[512,256,32]{1,2,0:T(8,128)(2,1)} %bitcast.40), calls=%async_computation.2 | async-start | bytes 16777216 | tf_op jit(solution)/shard_map/all_to_all | solution.py:44
Sparse Core Ops, SparseCore 0:
  9.5 201.5 all-gather.4
  212.7 198.8 all-gather.6
  486.5 198.9 all-gather.8
  725.7 357.3 all-gather.10
where the time goes:
time: 1190 us
  blocking collectives  571 us (48%)
  waiting for transfers between devices  313 us (26%)
  local copies, waits for them, and re-layouts  151 us (13%)
  matrix products  101 us (8%)
  other arithmetic  28 us (2%)
  between operations  14 us (1%)
    all_to_all x1, blocking collectives, shards(): lax.all_to_all(grad_second, 'chan', split_axis=2, concat_axis=1, tiled=True)  195 us
    all_gather x1, waiting for transfers between devices, shards(): lax.all_gather(second_mixing_blocks, 'chan', axis=1, tiled=True)  193 us
    all_to_all x1, blocking collectives, shards(): lax.all_to_all(grad_first_cols, 'seq', split_axis=2, concat_axis=0, tiled...  188 us
    all_to_all x1, blocking collectives, shards(): lax.all_to_all(first, 'seq', split_axis=0, concat_axis=2, tiled=True)  188 us
    all_to_all x1, waiting for transfers between devices, shards(): lax.all_to_all(grad_first, 'chan', split_axis=0, concat_axis=1, tiled=True)  119 us
    all_to_all x2, local copies, waits for them, and re-layouts, shards(): lax.all_to_all(grad_second, 'chan', split_axis=2, concat_axis=1, tiled=True)  30.8 us
    all_to_all x2, local copies, waits for them, and re-layouts, shards(): lax.all_to_all(grad_first, 'chan', split_axis=0, concat_axis=1, tiled=True)  30.6 us
    dot_general x1, matrix products, shards(): jnp.einsum('rgoi,godr->gdri', group_weight, group_grad, preferred_element...  26.4 us
  transfers between devices with their start and end apart: 5, of which 2 were waited for; matrix products, arithmetic and copies ran while one was open for 16% of the time, Pallas kernels for 0%

commit v1 on v0

--- a/solution.py
+++ b/solution.py
@@ -40,7 +40,12 @@
         jnp.einsum("cdo,cdi->coi", grad_second_rows, first_all, preferred_element_type=jnp.float32)
         * scale_two
     ).astype(jnp.bfloat16)
-    grad_first = lax.all_to_all(grad_first_cols, "seq", split_axis=2, concat_axis=0, tiled=True)
+    grad_first = jnp.concatenate(
+        lax.all_to_all(
+            jnp.stack(jnp.split(grad_first_cols, lax.axis_size("seq"), axis=2)), "seq", 0, 0
+        ),
+        axis=0,
+    )
     grad_part = lax.all_to_all(grad_first, "chan", split_axis=0, concat_axis=1, tiled=True)
     grad_mix_one = (
         jnp.einsum("odr,dri->roi", grad_part, gated_all, preferred_element_type=jnp.float32)

time: 1190 us -> 1240 us (1.042)
  blocking collectives: 571 us -> 418 us
  waiting for transfers between devices: 313 us -> 463 us
  local copies, waits for them, and re-layouts: 151 us -> 201 us
    all_to_all x1 -> x0, blocking collectives: 188 us -> none  [shards(): lax.all_to_all(grad_first_cols, 'seq', split_axis=2, concat_axis=0, tiled...]
    all_gather x1, waiting for transfers between devices: 0.01 us -> 104 us  [shards(): lax.all_gather(mix_one, 'chan', axis=1, tiled=True)]
    another operation x0 -> x18, local copies, waits for them, and re-layouts: none -> 53.1 us  [shards(): jnp.stack(jnp.split(grad_first_cols, lax.axis_size('seq'), axis=2))]
    all_to_all x0 -> x1, waiting for transfers between devices: none -> 45.8 us  [shards(): lax.all_to_all(jnp.stack(jnp.split(grad_first_cols, lax.axis_size('seq'),...]
    all_to_all x1, blocking collectives: 188 us -> 223 us  [shards(): lax.all_to_all(first, 'seq', split_axis=0, concat_axis=2, tiled=True)]
    unnamed x1 -> x22, local copies, waits for them, and re-layouts: 11.5 us -> 36.4 us
    convert_element_type x1 -> x0, local copies, waits for them, and re-layouts: 15.2 us -> none  [shards(): grad_first_cols = (jnp.einsum('coi,cdo->cdi', full_two, grad_second, pref...]
    all_to_all x1 -> x0, local copies, waits for them, and re-layouts: 12.5 us -> none  [shards(): lax.all_to_all(grad_first_cols, 'seq', split_axis=2, concat_axis=0, tiled...]
  transfers between devices with their start and end apart: 5 -> 6, of which waited for: 2 -> 4; matrix products, arithmetic and copies ran while one was open for 16% -> 19% of each run, Pallas kernels for 0% -> 0%
where the time goes in v1:
time: 1240 us; the launch traced here: 1230 us
  waiting for transfers between devices  463 us (37%)
  blocking collectives  418 us (34%)
  local copies, waits for them, and re-layouts  201 us (16%)
  matrix products  94.2 us (8%)
  other arithmetic  28 us (2%)
  between operations  14.1 us (1%)
  starting transfers between devices  13.4 us (1%)
    all_to_all x1, blocking collectives, shards(): lax.all_to_all(first, 'seq', split_axis=0, concat_axis=2, tiled=True)  223 us
    all_to_all x1, blocking collectives, shards(): lax.all_to_all(grad_second, 'chan', split_axis=2, concat_axis=1, tiled=True)  195 us
    all_gather x1, waiting for transfers between devices, shards(): lax.all_gather(second_mixing_blocks, 'chan', axis=1, tiled=True)  193 us
    all_to_all x1, waiting for transfers between devices, shards(): lax.all_to_all(grad_first, 'chan', split_axis=0, concat_axis=1, tiled=True)  119 us
    all_gather x1, waiting for transfers between devices, shards(): lax.all_gather(mix_one, 'chan', axis=1, tiled=True)  104 us
    another operation x18, local copies, waits for them, and re-layouts, shards(): jnp.stack(jnp.split(grad_first_cols, lax.axis_size('seq'), axis=2))  53.1 us
    all_to_all x1, waiting for transfers between devices, shards(): lax.all_to_all(jnp.stack(jnp.split(grad_first_cols, lax.axis_size('seq'),...  45.8 us
    unnamed x22, local copies, waits for them, and re-layouts  36.4 us
  transfers between devices with their start and end apart: 6, of which 4 were waited for; matrix products, arithmetic and copies ran while one was open for 19% of the time, Pallas kernels for 0%

profile of v1, /device:TPU:0, one launch (start us, length us, event | category | flops | bytes accessed | tf_op | source)
XLA Modules:
  0.0 1231.2 jit_solution(962697133572120252)
XLA Ops:
  8.6 9.9 fusion
  18.5 192.6 %all-gather.5.cloned.1.call-done = bf16[32,512,512]{2,1,0:T(8,128)(2,1)} async-done(((bf16[32,256,512]{2,1,0:T(8,128)(2,1)}), bf16[32,512,512]{2,1,0:T(8,128)(2,1)}) %all-gather.5.cloned.1.call-update) | async-done | bytes 16777232 | tf_op jit(solution)/shard_map/all_gather | solution.py:19
  211.1 11.8 multiply_convert_fusion.5
  222.9 16.3 %slice_bitcast_fusion = (bf16[1,32,256,32]{3,2,1,0:T(8,128)(2,1)}, bf16[1,32,256,32]{3,2,1,0:T(8,128)(2,1)}, bf16[1,32,256,32]{3,2,1,0:T(8,128)(2,1)}, bf16[1,32...) fusion(bf16[32,256,512]{2,1,0:T(8,128)(2,1)S(1)} %multiply_conv, ...), kind=kLoop, calls=%fused_computation.20 | loop fusion | bytes 16777216 | tf_op jit(solution)/shard_map/stack | solution.py:45
  239.3 2.2 copy.62
  241.5 2.0 copy.61
  243.5 2.6 copy.60
  246.1 2.6 copy.59
  250.2 2.7 copy.57
  252.9 2.6 copy.56
  255.5 2.6 copy.55
  258.0 1.9 constant_dynamic-update-slice_fusion.15
  259.9 1.9 constant_dynamic-update-slice_fusion.14
  261.8 1.9 constant_dynamic-update-slice_fusion.13
  263.7 1.9 constant_dynamic-update-slice_fusion.12
  265.5 1.9 constant_dynamic-update-slice_fusion.11
  267.4 1.9 constant_dynamic-update-slice_fusion.10
  271.7 2.0 copy.69
  273.7 2.6 copy.68
  276.3 2.6 copy.67
  278.9 2.6 copy.66
  281.5 2.6 copy.65
  284.0 2.6 copy.64
  290.0 1.9 constant_dynamic-update-slice_fusion.6
  291.8 1.9 constant_dynamic-update-slice_fusion.5
  297.4 1.9 constant_dynamic-update-slice_fusion.2
  301.0 5.8 all-to-all-start
  307.3 104.3 %all-gather.7.cloned.1.call-done = bf16[32,512,512]{2,1,0:T(8,128)(2,1)} async-done(((bf16[32,256,512]{2,1,0:T(8,128)(2,1)}), bf16[32,512,512]{2,1,0:T(8,128)(2,1)}) %all-gather.7.cloned.1.call-update) | async-done | bytes 16777232 | tf_op jit(solution)/shard_map/all_gather | solution.py:18
  411.5 45.8 %all-to-all-done = bf16[16,32,256,32]{2,3,1,0:T(8,128)(2,1)} async-done(((bf16[16,32,256,32]{2,3,1,0:T(8,128)(2,1)}), bf16[16,32,256,32]{2,3,1,0:T(8,128)(2,1)}, u32[]{:S(2)}, u32[]{:S(2)}) %all-to-all-start) | async-done | bytes 8388640 | tf_op jit(solution)/shard_map/all_to_all | solution.py:44
  457.3 25.9 %fusion.7 = bf16[32,256,512]{2,1,0:T(8,128)(2,1)} fusion(bf16[32,2,256,512]{3,2,1,0:T(8,128)(2,1)} %bitcast.71, bf16[2,256,256,32]{2,3,1,0:T(8,128)(2,1)} %bitcast.16), kind=kOutput, calls=%fused_computation.19 | convolution fusion | flops 4315938816 | bytes 33554432 | tf_op jit(solution)/shard_map/rgoi,godr->gdri/dot_general | solution.py:60
  483.2 18.1 %fusion.3 = (bf16[256,32,512]{2,0,1:T(8,128)(2,1)}, bf16[256,32,512]{2,0,1:T(8,128)(2,1)}) fusion(bf16[256,32,512]{2,1,0:T(8,128)(2,1)} %param.6, bf16[256,32,512]{2,1,0:T(8,128)(2,1)} %param.7, bf16[32,256,512]{2,1,0:T(8,128)(2,1)} %fusion.7), kind=kLoop, calls=%fused_computation.8 | loop fusion | flops 29360128 | bytes 41943040 | tf_op jit(solution)/shard_map/convert_element_type | solution.py:12
  501.4 13.1 %fusion.6 = bf16[512,256,32]{0,1,2:T(8,128)(2,1)} fusion(bf16[256,32,512]{2,0,1:T(8,128)(2,1)} %get-tuple-element.20, bf16[32,512,512]{2,1,0:T(8,128)(2,1)} %all-gather.7.cloned.1.call-done), kind=kOutput, calls=%fused_computation.18 | convolution fusion | flops 4303355904 | bytes 33554432 | tf_op jit(solution)/shard_map/roi,dri->odr/dot_general | solution.py:22
  514.5 14.6 %copy.75 = bf16[512,256,32]{1,2,0:T(8,128)(2,1)} copy(bf16[512,256,32]{0,1,2:T(8,128)(2,1)} %fusion.6) | data formatting | bytes 16777216 | tf_op jit(solution)/shard_map/convert_element_type | solution.py:24
  529.1 222.6 %all_to_all.59 = bf16[512,256,32]{1,2,0:T(8,128)(2,1)} all-to-all(bf16[512,256,32]{1,2,0:T(8,128)(2,1)} %copy.75), channel_id=1, replica_groups=mesh['seq'=16,'chan'=2] {'seq'}, dimensions={0} | all-to-all | bytes 16777216 | tf_op jit(solution)/shard_map/all_to_all | solution.py:25
  751.7 8.0 copy.76
  759.7 11.9 copy.81
  771.7 15.3 %copy.79 = bf16[32,256,512]{1,0,2:T(8,128)(2,1)} copy(bf16[32,256,512]{2,1,0:T(8,128)(2,1)} %fusion) | data formatting | bytes 16777216 | tf_op jit(solution)/shard_map/convert_element_type | solution.py:13
  787.0 195.0 %all_to_all.60 = bf16[32,256,512]{1,0,2:T(8,128)(2,1)} all-to-all(bf16[32,256,512]{1,0,2:T(8,128)(2,1)} %copy.79), channel_id=1, replica_groups=mesh['seq'=16,'chan'=2] {'chan'}, dimensions={2} | all-to-all | bytes 16777216 | tf_op jit(solution)/shard_map/all_to_all | solution.py:38
  982.0 7.0 all-to-all-start.2
  989.0 16.5 %copy.97 = bf16[32,256,2,256]{1,2,3,0:T(2,128)(2,1)} copy(bf16[32,256,2,256]{1,0,3,2:T(8,128)(2,1)} %bitcast.67) | data formatting | bytes 16777216 | tf_op jit(solution)/shard_map/all_to_all | solution.py:38
  1005.5 14.1 %all_to_all.54 = bf16[32,512,256]{1,2,0:T(8,128)(2,1)} reshape(bf16[32,2,256,256]{2,1,3,0:T(2,128)(2,1)} %bitcast.69) | data formatting | bytes 16777216 | tf_op jit(solution)/shard_map/all_to_all | solution.py:38
  1019.6 11.5 copy.82
  1031.1 119.3 %all-to-all-done.2 = bf16[512,256,32]{1,2,0:T(8,128)(2,1)} async-done(((bf16[512,256,32]{1,2,0:T(8,128)(2,1)}), bf16[512,256,32]{1,2,0:T(8,128)(2,1)}, u32[]{:S(2)}, u32[]{:S(2)}) %all-to-all-start.2) | async-done | bytes 8388640 | tf_op jit(solution)/shard_map/all_to_all | solution.py:49
  1150.4 16.5 %copy.98 = bf16[2,256,256,32]{2,0,1,3:T(2,128)(2,1)} copy(bf16[2,256,256,32]{2,3,1,0:T(8,128)(2,1)} %bitcast.24) | data formatting | bytes 16777216 | tf_op jit(solution)/shard_map/all_to_all | solution.py:49
  1166.9 14.0 %all_to_all.50 = bf16[256,512,32]{1,0,2:T(8,128)(2,1)} reshape(bf16[256,2,256,32]{2,1,0,3:T(2,128)(2,1)} %bitcast.70) | data formatting | bytes 16777216 | tf_op jit(solution)/shard_map/all_to_all | solution.py:49
  1181.0 15.6 %fusion.1 = bf16[32,256,512]{2,1,0:T(8,128)(2,1)} fusion(bf16[32,256,512]{2,1,0:T(8,128)(2,1)} %param.9, bf16[32,256,512]{1,2,0:T(8,128)(2,1)} %bitcast.66, bf16[32,512,512]{2,1,0:T(8,128)(2,1)} %all-gather.5.cloned.1.call-done), kind=kOutput, calls=%fused_computation.6 | convolution fusion | flops 4320133120 | bytes 41943040 | tf_op jit(solution)/shard_map/coi,cdi->cdo/dot_general | solution.py:28
  1196.6 14.0 %multiply_convert_fusion.2 = bf16[32,256,512]{2,1,0:T(8,128)(2,1)} fusion(bf16[256,512,32]{1,0,2:T(8,128)(2,1)} %all_to_all.50, bf16[512,32,512]{2,0,1:T(8,128)(2,1)} %all-gather.9.cloned.1.call-done), kind=kOutput, calls=%fused_computation.11 | convolution fusion | flops 4303355904 | bytes 33554432 | tf_op jit(solution)/shard_map/odr,dri->roi/dot_general | solution.py:51
  1210.6 13.8 %multiply_convert_fusion.1 = bf16[32,256,512]{2,1,0:T(8,128)(2,1)} fusion(bf16[32,512,256]{1,2,0:T(8,128)(2,1)} %all_to_all.54, bf16[32,512,512]{2,1,0:T(8,128)(2,1)} %all-gather.11.cloned.1.call-done), kind=kOutput, calls=%fused_computation.10 | convolution fusion | flops 4303355904 | bytes 33554432 | tf_op jit(solution)/shard_map/cdo,cdi->coi/dot_general | solution.py:40
  (26 shorter events, 14.7 us)
Async XLA Ops:
  7.2 204.0 %all-gather.5.cloned.1.call-start = ((), (), s32[]{:S(2)}) async-start(), calls=%async_computation.4 | async-start | bytes 25165824 | tf_op jit(solution)/shard_map/all_gather | solution.py:19
  7.9 403.7 %all-gather.7.cloned.1.call-start = ((), (), s32[]{:S(2)}) async-start(), calls=%async_computation.5 | async-start | bytes 25165824 | tf_op jit(solution)/shard_map/all_gather | solution.py:18
  239.3 9.4 copy-start.2
  250.2 20.7 %copy-start.1 = (bf16[1,32,256,32]{3,2,1,0:T(8,128)(2,1)S(1)}, bf16[1,32,256,32]{3,2,1,0:T(8,128)(2,1)}, u32[]{:S(2)}) copy-start(bf16[1,32,256,32]{3,2,1,0:T(8,128)(2,1)} %get-tuple-element.22) | copy-start | bytes 1572868
  271.7 14.9 %copy-start = (bf16[1,32,256,32]{3,2,1,0:T(8,128)(2,1)S(1)}, bf16[1,32,256,32]{3,2,1,0:T(8,128)(2,1)}, u32[]{:S(2)}) copy-start(bf16[1,32,256,32]{3,2,1,0:T(8,128)(2,1)} %get-tuple-element.29) | copy-start | bytes 1572868
  301.0 156.4 %all-to-all-start = ((bf16[16,32,256,32]{2,3,1,0:T(8,128)(2,1)}), bf16[16,32,256,32]{2,3,1,0:T(8,128)(2,1)}, u32[]{:S(2)}, u32[]{:S(2)}) async-start(bf16[16,32,256,32]{2,3,1,0:T(8,128)(2,1)} %constant_dynamic-update-slice_fusion), calls=%async_computation | async-start | bytes 16777216 | tf_op jit(solution)/shard_map/all_to_all | solution.py:44
  306.8 889.9 %all-gather.9.cloned.1.call-start = ((), (), s32[]{:S(2)}) async-start(), calls=%async_computation.6 | async-start | bytes 25165824 | tf_op jit(solution)/shard_map/all_gather | solution.py:16
  501.4 709.3 %all-gather.11.cloned.1.call-start = ((), (), s32[]{:S(2)}) async-start(), calls=%async_computation.7 | async-start | bytes 25165824 | tf_op jit(solution)/shard_map/all_gather | solution.py:26
  982.0 168.4 %all-to-all-start.2 = ((bf16[512,256,32]{1,2,0:T(8,128)(2,1)}), bf16[512,256,32]{1,2,0:T(8,128)(2,1)}, u32[]{:S(2)}, u32[]{:S(2)}) async-start(bf16[512,256,32]{1,2,0:T(8,128)(2,1)} %bitcast.23), calls=%async_computation.2 | async-start | bytes 16777216 | tf_op jit(solution)/shard_map/all_to_all | solution.py:49
Sparse Core Ops, SparseCore 0:
  9.5 201.5 all-gather.4
  212.7 198.8 all-gather.6
  501.5 229.9 all-gather.8
  771.8 357.3 all-gather.10
